TPU v7x, 32 devices: a whole 2x2x4 slice. The times are simulated.
32 devices in a mesh: dp: 2 (over x), seq: 16 (over z, y, core).
Axes of the slice: x: 2, y: 2, z: 4, core: 2. Of those that a mesh axis runs over, the one named last changes fastest.
Arguments:
- query: bfloat16 [2048, 3072], P('seq', 'dp'), may hold values from -300 to 300
- key: bfloat16 [2048, 3072], P('seq', 'dp'), may hold values from -10 to 10
- value: bfloat16 [2048, 3072], P('seq', 'dp'), may hold values from -6 to 6
- d_query: bfloat16 [2048, 3072], P('seq', 'dp'), may hold values from -6 to 6
- d_key: bfloat16 [2048, 3072], P('seq', 'dp'), may hold values from -6 to 6
- d_value: bfloat16 [2048, 3072], P('seq', 'dp'), may hold values from -6 to 6
- residual: bfloat16 [2048, 3072], P('seq', 'dp'), may hold values from -6 to 6
- d_residual: bfloat16 [2048, 3072], P('seq', 'dp'), may hold values from -6 to 6
- w_in: bfloat16 [3072, 7168], P('seq', 'dp'), may hold values from -0.109375 to 0.109375
- w_out: bfloat16 [7168, 3072], P(('dp', 'seq')), may hold values from -0.125 to 0.125
Outputs:
- block_out: bfloat16 [2048, 3072], P('seq', 'dp')
- d_block_out: bfloat16 [2048, 3072], P('seq', 'dp')
All inputs are finite; a program needn't handle non-finite values.
Results may differ from a plain program's by a relative error of at most 0.025.
Values may be sent and summed in bfloat16 or wider, within the bound.
A program may use at most 192 MiB of HBM per device.

v0:
```python
import math
import jax
import jax.numpy as jnp
from jax import lax
from jax.sharding import PartitionSpec as P

HEAD_DIM = 128
gelu_coeff = 0.7978845608
cubic_coeff = 0.044715


def gelu_pair(pre_act, d_pre_act):
    inner_arg = gelu_coeff * (pre_act + cubic_coeff * pre_act * pre_act * pre_act)
    hyper = jnp.tanh(inner_arg)
    gelu_value = 0.5 * pre_act * (1.0 + hyper)
    gelu_slope = 0.5 * (1.0 + hyper) + 0.5 * pre_act * (1.0 - hyper * hyper) * gelu_coeff * (
        1.0 + 3.0 * cubic_coeff * pre_act * pre_act
    )
    return (gelu_value, gelu_slope * d_pre_act)


def on_device(query, key, value, d_query, d_key, d_value, residual, d_residual, w_in, w_out):
    row_count = query.shape[0]
    feat_width = query.shape[1]
    head_count = feat_width // HEAD_DIM
    score_scale = 1.0 / math.sqrt(HEAD_DIM)
    query_heads = query.reshape(row_count, head_count, HEAD_DIM)
    dquery_heads = d_query.reshape(row_count, head_count, HEAD_DIM)
    pieces = (
        lax.all_gather(key, "seq", axis=0, tiled=True),
        lax.all_gather(value, "seq", axis=0, tiled=True),
        lax.all_gather(d_key, "seq", axis=0, tiled=True),
        lax.all_gather(d_value, "seq", axis=0, tiled=True),
    )
    run_peak = jnp.full((head_count, row_count), -1e30, jnp.float32)
    key_heads, value_heads, dkey_heads, dvalue_heads = tuple(
        (piece.reshape(piece.shape[0], head_count, HEAD_DIM) for piece in pieces)
    )
    scores = (
        jnp.einsum("qhd,khd->hqk", query_heads, key_heads, preferred_element_type=jnp.float32)
        * score_scale
    )
    d_scores = (
        jnp.einsum("qhd,khd->hqk", dquery_heads, key_heads, preferred_element_type=jnp.float32)
        + jnp.einsum("qhd,khd->hqk", query_heads, dkey_heads, preferred_element_type=jnp.float32)
    ) * score_scale
    new_peak = jnp.maximum(run_peak, jnp.max(scores, axis=2))
    weights = jnp.exp(scores - new_peak[:, :, None])
    mixed = weights * d_scores
    weights_low = weights.astype(jnp.bfloat16)
    mixed_low = mixed.astype(jnp.bfloat16)
    new_total = jnp.sum(weights, axis=2)
    new_slope = jnp.sum(mixed, axis=2)
    new_accum = jnp.einsum(
        "hqk,khd->hqd", weights_low, value_heads, preferred_element_type=jnp.float32
    )
    new_tangent = jnp.einsum(
        "hqk,khd->hqd", mixed_low, value_heads, preferred_element_type=jnp.float32
    ) + jnp.einsum("hqk,khd->hqd", weights_low, dvalue_heads, preferred_element_type=jnp.float32)
    attended = new_accum / new_total[:, :, None]
    d_attended = (
        new_tangent / new_total[:, :, None] - (new_slope / new_total)[:, :, None] * attended
    )
    attended = attended.transpose(1, 0, 2).reshape(row_count, feat_width)
    d_attended = d_attended.transpose(1, 0, 2).reshape(row_count, feat_width)
    mixed_in = (residual.astype(jnp.float32) + attended).astype(jnp.bfloat16)
    d_mixed_in = (d_residual.astype(jnp.float32) + d_attended).astype(jnp.bfloat16)
    w_in_whole, w_out_whole = (
        lax.all_gather(w_in, "seq", axis=0, tiled=True),
        lax.all_gather(w_out, "seq", axis=0, tiled=True),
    )
    whole_in, d_whole_in = (
        lax.all_gather(mixed_in, "dp", axis=1, tiled=True),
        lax.all_gather(d_mixed_in, "dp", axis=1, tiled=True),
    )
    pre_act = jnp.dot(whole_in, w_in_whole, preferred_element_type=jnp.float32)
    d_pre_act = jnp.dot(d_whole_in, w_in_whole, preferred_element_type=jnp.float32)
    hidden, d_hidden = gelu_pair(pre_act, d_pre_act)
    hidden = hidden.astype(jnp.bfloat16)
    d_hidden = d_hidden.astype(jnp.bfloat16)
    partial_value = jnp.dot(hidden, w_out_whole, preferred_element_type=jnp.float32)
    d_partial = jnp.dot(d_hidden, w_out_whole, preferred_element_type=jnp.float32)
    summed, d_summed = (
        lax.psum_scatter(
            partial_value.astype(jnp.bfloat16), "dp", scatter_dimension=1, tiled=True
        ).astype(jnp.float32),
        lax.psum_scatter(
            d_partial.astype(jnp.bfloat16), "dp", scatter_dimension=1, tiled=True
        ).astype(jnp.float32),
    )
    block_out = (mixed_in.astype(jnp.float32) + summed).astype(jnp.bfloat16)
    d_block_out = (d_mixed_in.astype(jnp.float32) + d_summed).astype(jnp.bfloat16)
    return (block_out, d_block_out)


def solution(mesh):
    in_specs = (
        P("seq", "dp"),
        P("seq", "dp"),
        P("seq", "dp"),
        P("seq", "dp"),
        P("seq", "dp"),
        P("seq", "dp"),
        P("seq", "dp"),
        P("seq", "dp"),
        P("seq", "dp"),
        P(("dp", "seq"), None),
    )
    out_specs = (P("seq", "dp"), P("seq", "dp"))
    return jax.shard_map(
        on_device, mesh=mesh, in_specs=in_specs, out_specs=out_specs, check_vma=False
    )
```

profile of v0, /device:TPU:0, one launch (start us, length us, event | category | flops | bytes accessed | tf_op | source)
XLA Modules:
  0.0 555.8 jit_solution(12770551989080818743)
XLA Ops:
  7.2 0.0 all-gather.9.cloned.1.call-start
  7.2 0.7 all-gather.9.cloned.1.call-update
  7.9 0.0 all-gather.17.cloned.1.call-start
  8.0 0.7 all-gather.17.cloned.1.call-update
  8.7 0.0 all-gather.7.cloned.1.call-start
  8.7 1.9 copy.20
  10.6 0.0 all-gather.7.cloned.1.call-update
  10.6 0.0 all-gather.15.cloned.1.call-start
  10.7 1.9 copy.28
  12.6 0.0 all-gather.11.cloned.1.call-start
  12.7 0.5 all-gather.11.cloned.1.call-update
  13.2 0.0 all-gather.13.cloned.1.call-start
  13.3 0.5 all-gather.13.cloned.1.call-update
  13.8 0.0 reduce-scatter.5.cloned.1.call-start
  13.8 1.2 copy.19
  15.1 0.2 copy.25
  15.3 59.1 %all-gather.9.cloned.1.call-done = bf16[2048,1536]{1,0:T(8,128)(2,1)} async-done(((bf16[128,1536]{1,0:T(8,128)(2,1)}), bf16[2048,1536]{1,0:T(8,128)(2,1)}) %all-gather.9.cloned.1.call-update) | async-done | bytes 6291472 | tf_op jit(solution)/shard_map/all_gather | solution.py:31
  74.4 8.7 %copy.23 = bf16[2048,1536]{0,1:T(8,128)(2,1)} copy(bf16[2048,1536]{1,0:T(8,128)(2,1)} %all-gather.9.cloned.1.call-done) | data formatting | bytes 12582912 | tf_op jit(solution)/shard_map/all_gather | solution.py:31
  83.1 53.7 %all-gather.17.cloned.1.call-done = bf16[2048,1536]{1,0:T(8,128)(2,1)} async-done(((bf16[128,1536]{1,0:T(8,128)(2,1)}), bf16[2048,1536]{1,0:T(8,128)(2,1)}) %all-gather.17.cloned.1.call-update) | async-done | bytes 6291472 | tf_op jit(solution)/shard_map/all_gather | solution.py:33
  136.8 8.7 %copy.31 = bf16[2048,1536]{0,1:T(8,128)(2,1)} copy(bf16[2048,1536]{1,0:T(8,128)(2,1)} %all-gather.17.cloned.1.call-done) | data formatting | bytes 12582912 | tf_op jit(solution)/shard_map/all_gather | solution.py:33
  145.5 58.0 %all-gather.7.cloned.1.call-done = bf16[2048,1536]{0,1:T(8,128)(2,1)} async-done(((bf16[128,1536]{0,1:T(8,128)(2,1)}), bf16[2048,1536]{0,1:T(8,128)(2,1)}) %all-gather.7.cloned.1.call-update) | async-done | bytes 6291472 | tf_op jit(solution)/shard_map/all_gather | solution.py:30
  203.6 4.9 multiply_reduce_fusion
  208.5 6.8 %fusion.38 = f32[12,128,2048]{2,1,0:T(8,128)} fusion(bf16[128,12,128]{0,2,1:T(8,128)(2,1)S(1)} %bitcast.51, bf16[2048,12,128]{0,2,1:T(8,128)(2,1)S(1)} %bitcast.42), kind=kOutput, calls=%fused_computation.44 | convolution fusion | flops 805306368 | bytes 19267584 | tf_op jit(solution)/shard_map/qhd,khd->hqk/dot_general | solution.py:44
  215.3 1.5 copy-done
  216.8 2.4 fusion
  219.3 50.4 %all-gather.15.cloned.1.call-done = bf16[2048,1536]{0,1:T(8,128)(2,1)} async-done(((bf16[128,1536]{0,1:T(8,128)(2,1)}), bf16[2048,1536]{0,1:T(8,128)(2,1)}) %all-gather.15.cloned.1.call-update) | async-done | bytes 6291472 | tf_op jit(solution)/shard_map/all_gather | solution.py:32
  269.6 16.3 %fusion.36 = (f32[12,128]{1,0:T(8,128)S(1)}, bf16[12,128,2048]{2,1,0:T(8,128)(2,1)}) fusion(f32[12,128,2048]{2,1,0:T(8,128)} %fusion.38, bf16[128,12,128]{0,2,1:T(8,128)(2,1)S(1)} %bitcast.50, bf16[2048,12,128]{0,2,1:T(8,128)(2,1)} %bitcast.48, f32[12,128]{1,0:T(8,128)S(1)} %broadcast_maximum_fusion, f32[12,128,2048]{2,1,0:T(8,128)} %copy-done), kind=kOutput, calls=%fused_computation.42 | convolution fusion | flops 827324928 | bytes 38154240 | tf_op jit(solution)/shard_map/qhd,khd->hqk/dot_general | solution.py:45
  286.0 6.6 %fusion.27 = f32[12,128,128]{1,2,0:T(8,128)S(1)} fusion(bf16[2048,12,128]{0,2,1:T(8,128)(2,1)S(1)} %bitcast.45, f32[12,128,2048]{2,1,0:T(8,128)} %copy-done, f32[12,128]{1,0:T(8,128)S(1)} %broadcast_maximum_fusion), kind=kOutput, calls=%fused_computation.29 | convolution fusion | flops 814743552 | bytes 19666944 | tf_op jit(solution)/shard_map/hqk,khd->hqd/dot_general | solution.py:59
  292.6 10.5 %fusion.22 = f32[128,12,128]{0,2,1:T(8,128)} fusion(bf16[2048,12,128]{0,2,1:T(8,128)(2,1)} %bitcast.46, f32[12,128,2048]{2,1,0:T(8,128)} %copy-done, f32[12,128]{1,0:T(8,128)S(1)} %broadcast_maximum_fusion, f32[128,12]{0,1:T(8,128)S(1)} %bitcast.54), kind=kOutput, calls=%fused_computation.24 | convolution fusion | flops 814940160 | bytes 19673088 | tf_op jit(solution)/shard_map/hqk,khd->hqd/dot_general | solution.py:54
  303.1 6.2 %fusion.19 = f32[128,12,128]{0,2,1:T(8,128)} fusion(f32[12,128,128]{1,2,0:T(8,128)S(1)} %fusion.27, bf16[2048,12,128]{0,2,1:T(8,128)(2,1)} %bitcast.47, bf16[12,128,2048]{2,1,0:T(8,128)(2,1)S(1)} %copy-done.2, f32[128,12,128]{0,2,1:T(8,128)} %fusion.22, f32[128,12]{0,1:T(8,128)S(1)} %bitcast_divide_fusion, f32[128,12]{0,1:T(8,128)S(1)} %bitcast.55), kind=kOutput, calls=%fused_computation.23 | convolution fusion | flops 806092800 | bytes 14954496 | tf_op jit(solution)/shard_map/hqk,khd->hqd/dot_general | solution.py:57
  309.3 1.4 copy.32
  310.7 1.4 copy.24
  312.1 0.1 add_convert_fusion.1
  312.2 11.9 %all_gather.31 = bf16[128,3072]{1,0:T(8,128)(2,1)} all-gather(bf16[128,1536]{1,0:T(8,128)(2,1)S(1)} %add_convert_fusion.1), channel_id=1, replica_groups=mesh['dp'=2,'seq'=16] {'dp'}, dimensions={1}, use_global_device_ids=true | all-gather | bytes 1179648 | tf_op jit(solution)/shard_map/all_gather | solution.py:74
  324.0 0.1 add_convert_fusion.3
  324.1 10.9 %all_gather.26 = bf16[128,3072]{1,0:T(8,128)(2,1)S(1)} all-gather(bf16[128,1536]{1,0:T(8,128)(2,1)S(1)} %add_convert_fusion.3), channel_id=1, replica_groups=mesh['dp'=2,'seq'=16] {'dp'}, dimensions={1}, use_global_device_ids=true | all-gather | bytes 1179648 | tf_op jit(solution)/shard_map/all_gather | solution.py:73
  335.0 47.9 %all-gather.11.cloned.1.call-done = bf16[3072,3584]{1,0:T(8,128)(2,1)} async-done(((bf16[192,3584]{1,0:T(8,128)(2,1)}), bf16[3072,3584]{1,0:T(8,128)(2,1)}) %all-gather.11.cloned.1.call-update) | async-done | bytes 22020112 | tf_op jit(solution)/shard_map/all_gather | solution.py:69
  383.0 11.7 %fusion.37 = f32[128,3584]{1,0:T(8,128)} fusion(bf16[128,3072]{1,0:T(8,128)(2,1)S(1)} %all_gather.26, bf16[3072,3584]{1,0:T(8,128)(2,1)} %all-gather.11.cloned.1.call-done), kind=kOutput, calls=%fused_computation.43 | convolution fusion | flops 2818572288 | bytes 24641536 | tf_op jit(solution)/shard_map/dot_general | solution.py:76
  394.7 3.4 copy-done.1
  398.1 6.5 %fusion.4 = bf16[128,3584]{1,0:T(8,128)(2,1)} fusion(bf16[128,3072]{1,0:T(8,128)(2,1)} %all_gather.31, bf16[3072,3584]{1,0:T(8,128)(2,1)S(1)} %copy-done.1, f32[128,3584]{1,0:T(8,128)} %fusion.37), kind=kOutput, calls=%fused_computation.8 | convolution fusion | flops 2827288576 | bytes 25559040 | tf_op jit(solution)/shard_map/dot_general | solution.py:77
  404.6 93.6 %all-gather.13.cloned.1.call-done = bf16[3584,3072]{1,0:T(8,128)(2,1)} async-done(((bf16[224,3072]{1,0:T(8,128)(2,1)}), bf16[3584,3072]{1,0:T(8,128)(2,1)}) %all-gather.13.cloned.1.call-update) | async-done | bytes 22020112 | tf_op jit(solution)/shard_map/all_gather | solution.py:70
  498.2 11.5 %convolution_convert_fusion = bf16[128,3072]{1,0:T(8,128)(2,1)} fusion(bf16[128,3584]{1,0:T(8,128)(2,1)} %fusion.4, bf16[3584,3072]{1,0:T(8,128)(2,1)} %all-gather.13.cloned.1.call-done), kind=kOutput, calls=%fused_computation.9 | convolution fusion | flops 2818965504 | bytes 23724032 | tf_op jit(solution)/shard_map/dot_general | solution.py:82
  509.7 0.0 reduce-scatter.3.cloned.1.call-start
  509.7 11.7 %convolution_convert_fusion.1 = bf16[128,3072]{1,0:T(8,128)(2,1)} fusion(bf16[3584,3072]{1,0:T(8,128)(2,1)} %all-gather.13.cloned.1.call-done, f32[128,3584]{1,0:T(8,128)S(1)} %copy-done.3), kind=kOutput, calls=%fused_computation.10 | convolution fusion | flops 2823094272 | bytes 24641536 | tf_op jit(solution)/shard_map/dot_general | solution.py:81
  521.4 5.9 %reduce-scatter.5.cloned.1.call-done = bf16[128,1536]{1,0:T(8,128)(2,1)} async-done(((bf16[128,3072]{1,0:T(8,128)(2,1)}), bf16[128,1536]{1,0:T(8,128)(2,1)}) %reduce-scatter.5.cloned.1.call-update) | async-done | bytes 393232 | tf_op jit(solution)/shard_map/reduce_scatter | solution.py:87
  527.3 1.8 add_convert_fusion
  529.1 18.0 %reduce-scatter.3.cloned.1.call-done = bf16[128,1536]{1,0:T(8,128)(2,1)} async-done(((bf16[128,3072]{1,0:T(8,128)(2,1)}), bf16[128,1536]{1,0:T(8,128)(2,1)}) %reduce-scatter.3.cloned.1.call-update) | async-done | bytes 393232 | tf_op jit(solution)/shard_map/reduce_scatter | solution.py:84
  547.1 1.8 add_convert_fusion.2
  (27 shorter events, 0.1 us)
Async XLA Ops:
  7.2 7.9 %copy-start.4 = (bf16[128,1536]{1,0:T(8,128)(2,1)S(1)}, bf16[128,1536]{1,0:T(8,128)(2,1)}, u32[]{:S(2)}) copy-start(bf16[128,1536]{1,0:T(8,128)(2,1)} %param.13) | copy-start | bytes 1179652
  7.2 67.2 %all-gather.9.cloned.1.call-start = ((), (), s32[]{:S(2)}) async-start(), calls=%async_computation.3 | async-start | bytes 6684672 | tf_op jit(solution)/shard_map/all_gather | solution.py:31
  7.9 128.9 %all-gather.17.cloned.1.call-start = ((), (), s32[]{:S(2)}) async-start(), calls=%async_computation.8 | async-start | bytes 6684672 | tf_op jit(solution)/shard_map/all_gather | solution.py:33
  8.7 194.9 %all-gather.7.cloned.1.call-start = ((), (), s32[]{:S(2)}) async-start(), calls=%async_computation.2 | async-start | bytes 6684672 | tf_op jit(solution)/shard_map/all_gather | solution.py:30
  10.6 259.0 %all-gather.15.cloned.1.call-start = ((), (), s32[]{:S(2)}) async-start(), calls=%async_computation.7 | async-start | bytes 6684672 | tf_op jit(solution)/shard_map/all_gather | solution.py:32
  12.6 370.3 %all-gather.11.cloned.1.call-start = ((), (), s32[]{:S(2)}) async-start(), calls=%async_computation.4 | async-start | bytes 23396352 | tf_op jit(solution)/shard_map/all_gather | solution.py:69
  13.2 484.9 %all-gather.13.cloned.1.call-start = ((), (), s32[]{:S(2)}) async-start(), calls=%async_computation.5 | async-start | bytes 23396352 | tf_op jit(solution)/shard_map/all_gather | solution.py:70
  13.8 513.5 %reduce-scatter.5.cloned.1.call-start = ((), (), s32[]{:S(2)}) async-start(), calls=%async_computation.9 | async-start | bytes 1179648 | tf_op jit(solution)/shard_map/reduce_scatter | solution.py:87
  203.6 4.9 slice-start
  203.6 4.9 slice-start.1
  208.4 8.4 %copy-start = (f32[12,128,2048]{2,1,0:T(8,128)}, f32[12,128,2048]{2,1,0:T(8,128)S(1)}, u32[]{:S(2)}) copy-start(f32[12,128,2048]{2,1,0:T(8,128)S(1)} %get-tuple-element.3) | copy-start | bytes 37748740
  216.8 69.1 %slice-start.2 = ((s8[6291456]{0:T(1024)(128)(4,1)}), s8[2097152]{0:T(1024)(128)(4,1)S(1)}, s32[]{:S(2)}) async-start(s8[6291456]{0:T(1024)(128)(4,1)} %bitcast.43), calls=%async_computation.12 | async-start | bytes 4194304
  269.6 16.3 %slice-start.3 = ((s8[6291456]{0:T(1024)(128)(4,1)}), s8[4194304]{0:T(1024)(128)(4,1)S(1)}, s32[]{:S(2)}) async-start(s8[6291456]{0:T(1024)(128)(4,1)} %bitcast.43), calls=%async_computation.13 | async-start | bytes 8388608
  292.5 10.5 %copy-start.2 = (bf16[12,128,2048]{2,1,0:T(8,128)(2,1)S(1)}, bf16[12,128,2048]{2,1,0:T(8,128)(2,1)}, u32[]{:S(2)}) copy-start(bf16[12,128,2048]{2,1,0:T(8,128)(2,1)} %get-tuple-element.5) | copy-start | bytes 18874372
  303.1 9.0 %copy-start.5 = (bf16[128,1536]{1,0:T(8,128)(2,1)S(1)}, bf16[128,1536]{1,0:T(8,128)(2,1)}, u32[]{:S(2)}) copy-start(bf16[128,1536]{1,0:T(8,128)(2,1)} %param.17) | copy-start | bytes 1179652
  303.1 21.0 %copy-start.6 = (bf16[128,1536]{1,0:T(8,128)(2,1)S(1)}, bf16[128,1536]{1,0:T(8,128)(2,1)}, u32[]{:S(2)}) copy-start(bf16[128,1536]{1,0:T(8,128)(2,1)} %param.16) | copy-start | bytes 1179652
  383.0 15.1 %copy-start.1 = (bf16[3072,3584]{1,0:T(8,128)(2,1)S(1)}, bf16[3072,3584]{1,0:T(8,128)(2,1)}, u32[]{:S(2)}) copy-start(bf16[3072,3584]{1,0:T(8,128)(2,1)} %all-gather.11.cloned.1.call-done) | copy-start | bytes 66060292
  404.6 105.1 %copy-start.3 = (f32[128,3584]{1,0:T(8,128)S(1)}, f32[128,3584]{1,0:T(8,128)}, u32[]{:S(2)}) copy-start(f32[128,3584]{1,0:T(8,128)} %fusion.37) | copy-start | bytes 5505028
  509.7 37.5 %reduce-scatter.3.cloned.1.call-start = ((), (), s32[]{:S(2)}) async-start(), calls=%async_computation.6 | async-start | bytes 1179648 | tf_op jit(solution)/shard_map/reduce_scatter | solution.py:84
Sparse Core Ops, SparseCore 0:
  10.3 64.1 all-gather.8
  76.7 60.0 all-gather.16
  139.6 63.9 all-gather.6
  206.1 63.4 all-gather.14
  271.1 111.8 all-gather.10
  384.4 113.6 all-gather.12
  509.8 17.4 reduce-scatter.4
  529.5 17.5 reduce-scatter.2
where the time goes:
time: 557 us; the launch traced here: 556 us
  waiting for transfers between devices  389 us (70%)
  matrix products  92.6 us (17%)
  local copies, waits for them, and re-layouts  30.4 us (5%)
  blocking collectives  22.8 us (4%)
  between operations  14.3 us (3%)
  other arithmetic  6.27 us (1%)
    all_gather x1, waiting for transfers between devices, on_device(): lax.all_gather(w_out, 'seq', axis=0, tiled=True)  93.6 us
    all_gather x1, waiting for transfers between devices, on_device(): lax.all_gather(value, 'seq', axis=0, tiled=True)  59.1 us
    all_gather x1, waiting for transfers between devices, on_device(): lax.all_gather(key, 'seq', axis=0, tiled=True)  58 us
    all_gather x1, waiting for transfers between devices, on_device(): lax.all_gather(d_value, 'seq', axis=0, tiled=True)  53.7 us
    all_gather x1, waiting for transfers between devices, on_device(): lax.all_gather(d_key, 'seq', axis=0, tiled=True)  50.4 us
    all_gather x1, waiting for transfers between devices, on_device(): lax.all_gather(w_in, 'seq', axis=0, tiled=True)  47.9 us
    reduce_scatter x1, waiting for transfers between devices, on_device(): lax.psum_scatter(partial_value.astype(jnp.bfloat16), 'dp', scatter_dimens...  18 us
    dot_general x1, matrix products, on_device(): jnp.einsum('qhd,khd->hqk', query_heads, dkey_heads, preferred_element_typ...  16.3 us
  transfers between devices with their start and end apart: 8, of which 8 were waited for; matrix products, arithmetic and copies ran while one was open for 20% of the time, Pallas kernels for 0%

commit v1 on v0

--- a/solution.py
+++ b/solution.py
@@ -28,7 +28,9 @@
     dquery_heads = d_query.reshape(row_count, head_count, HEAD_DIM)
     pieces = (
         lax.all_gather(key, "seq", axis=0, tiled=True),
-        lax.all_gather(value, "seq", axis=0, tiled=True),
+        jnp.concatenate(
+            lax.all_to_all(jnp.stack([value] * lax.axis_size("seq")), "seq", 0, 0), axis=0
+        ),
         lax.all_gather(d_key, "seq", axis=0, tiled=True),
         lax.all_gather(d_value, "seq", axis=0, tiled=True),
     )

time: 557 us -> 592 us (1.063)
  local copies, waits for them, and re-layouts: 30.4 us -> 44.7 us
  waiting for transfers between devices: 389 us -> 403 us
  starting transfers between devices: 0.32 us -> 7.87 us
    all_to_all x0 -> x1, waiting for transfers between devices: none -> 158 us  [on_device(): lax.all_to_all(jnp.stack([value] * lax.axis_size('seq')), 'seq', 0, 0)]
    all_gather x1 -> x0, waiting for transfers between devices: 59.1 us -> none  [on_device(): lax.all_gather(value, 'seq', axis=0, tiled=True)]
    all_gather x1, waiting for transfers between devices: 53.7 us -> 0.01 us  [on_device(): lax.all_gather(d_value, 'seq', axis=0, tiled=True)]
    all_gather x1, waiting for transfers between devices: 58 us -> 26.4 us  [on_device(): lax.all_gather(key, 'seq', axis=0, tiled=True)]
    another operation x0 -> x2, local copies, waits for them, and re-layouts: none -> 14.3 us  [the longest x1 10.4 us: on_device(): piece.reshape(piece.shape[0], head_count, HEAD_DIM)]
    all_gather x1 -> x0, local copies, waits for them, and re-layouts: 8.7 us -> none  [on_device(): lax.all_gather(value, 'seq', axis=0, tiled=True)]
    all_to_all x0 -> x1, local copies, waits for them, and re-layouts: none -> 8.51 us  [on_device(): lax.all_to_all(jnp.stack([value] * lax.axis_size('seq')), 'seq', 0, 0)]
    all_to_all x0 -> x1, starting transfers between devices: none -> 7.59 us  [on_device(): lax.all_to_all(jnp.stack([value] * lax.axis_size('seq')), 'seq', 0, 0)]
  transfers between devices with their start and end apart: 8 -> 8, of which waited for: 8 -> 7; matrix products, arithmetic and copies ran while one was open for 20% -> 21% of each run, Pallas kernels for 0% -> 0%
where the time goes in v1:
time: 592 us; the launch traced here: 591 us
  waiting for transfers between devices  403 us (68%)
  matrix products  92.6 us (16%)
  local copies, waits for them, and re-layouts  44.7 us (8%)
  blocking collectives  22.8 us (4%)
  between operations  14.3 us (2%)
  starting transfers between devices  7.87 us (1%)
  other arithmetic  6.27 us (1%)
    all_to_all x1, waiting for transfers between devices, on_device(): lax.all_to_all(jnp.stack([value] * lax.axis_size('seq')), 'seq', 0, 0)  158 us
    all_gather x1, waiting for transfers between devices, on_device(): lax.all_gather(w_out, 'seq', axis=0, tiled=True)  93.6 us
    all_gather x1, waiting for transfers between devices, on_device(): lax.all_gather(d_key, 'seq', axis=0, tiled=True)  51.3 us
    all_gather x1, waiting for transfers between devices, on_device(): lax.all_gather(w_in, 'seq', axis=0, tiled=True)  48 us
    all_gather x1, waiting for transfers between devices, on_device(): lax.all_gather(key, 'seq', axis=0, tiled=True)  26.4 us
    reduce_scatter x1, waiting for transfers between devices, on_device(): lax.psum_scatter(partial_value.astype(jnp.bfloat16), 'dp', scatter_dimens...  18 us
    dot_general x1, matrix products, on_device(): jnp.einsum('qhd,khd->hqk', query_heads, dkey_heads, preferred_element_typ...  16.3 us
    all_gather x1, blocking collectives, on_device(): lax.all_gather(d_mixed_in, 'dp', axis=1, tiled=True)  11.9 us
  transfers between devices with their start and end apart: 8, of which 7 were waited for; matrix products, arithmetic and copies ran while one was open for 21% of the time, Pallas kernels for 0%

profile of v1, /device:TPU:0, one launch (start us, length us, event | category | flops | bytes accessed | tf_op | source)
XLA Modules:
  0.0 591.2 jit_solution(7264643166093638865)
XLA Ops:
  7.2 0.0 all-gather.14.cloned.1.call-start
  7.2 0.7 all-gather.14.cloned.1.call-update
  7.9 0.0 all-gather.6.cloned.1.call-start
  7.9 1.9 copy.34
  9.9 0.0 all-gather.12.cloned.1.call-start
  9.9 1.9 copy.43
  11.9 0.0 all-gather.8.cloned.1.call-start
  11.9 0.5 all-gather.8.cloned.1.call-update
  12.5 0.0 all-gather.10.cloned.1.call-start
  12.5 0.5 all-gather.10.cloned.1.call-update
  13.0 1.2 copy.37
  14.3 3.8 stack.2
  18.1 7.6 %all-to-all-start = ((bf16[16,128,1536]{1,2,0:T(8,128)(2,1)}), bf16[16,128,1536]{1,2,0:T(8,128)(2,1)}, u32[]{:S(2)}, u32[]{:S(2)}) async-start(bf16[16,128,1536]{1,2,0:T(8,128)(2,1)} %stack.2), calls=%async_computation | async-start | bytes 12582912 | tf_op jit(solution)/shard_map/all_to_all | solution.py:32
  25.7 0.0 reduce-scatter.5.cloned.1.call-start
  25.8 0.2 copy.33
  26.0 0.2 copy.40
  26.2 157.7 %all-to-all-done = bf16[16,128,1536]{1,2,0:T(8,128)(2,1)} async-done(((bf16[16,128,1536]{1,2,0:T(8,128)(2,1)}), bf16[16,128,1536]{1,2,0:T(8,128)(2,1)}, u32[]{:S(2)}, u32[]{:S(2)}) %all-to-all-start) | async-done | bytes 6291488 | tf_op jit(solution)/shard_map/all_to_all | solution.py:32
  183.9 8.5 %copy.38 = bf16[16,128,1536]{1,0,2:T(8,128)(2,1)} copy(bf16[16,128,1536]{1,2,0:T(8,128)(2,1)} %all-to-all-done) | data formatting | bytes 12582912 | tf_op jit(solution)/shard_map/all_to_all | solution.py:32
  192.4 10.4 %reshape_reshape.3 = bf16[2048,12,128]{0,2,1:T(8,128)(2,1)} reshape(bf16[16,128,1536]{1,0,2:T(8,128)(2,1)} %copy.38) | data formatting | bytes 12582912 | tf_op jit(solution)/shard_map/reshape;reshape | solution.py:39
  202.8 8.7 %copy.46 = bf16[2048,1536]{0,1:T(8,128)(2,1)} copy(bf16[2048,1536]{1,0:T(8,128)(2,1)} %all-gather.14.cloned.1.call-done) | data formatting | bytes 12582912 | tf_op jit(solution)/shard_map/all_gather | solution.py:35
  211.6 26.4 %all-gather.6.cloned.1.call-done = bf16[2048,1536]{0,1:T(8,128)(2,1)} async-done(((bf16[128,1536]{0,1:T(8,128)(2,1)}), bf16[2048,1536]{0,1:T(8,128)(2,1)}) %all-gather.6.cloned.1.call-update) | async-done | bytes 6291472 | tf_op jit(solution)/shard_map/all_gather | solution.py:30
  237.9 4.9 multiply_reduce_fusion
  242.9 6.8 %fusion.38 = f32[12,128,2048]{2,1,0:T(8,128)} fusion(bf16[128,12,128]{0,2,1:T(8,128)(2,1)S(1)} %bitcast.50, bf16[2048,12,128]{0,2,1:T(8,128)(2,1)S(1)} %bitcast.43), kind=kOutput, calls=%fused_computation.44 | convolution fusion | flops 805306368 | bytes 19267584 | tf_op jit(solution)/shard_map/qhd,khd->hqk/dot_general | solution.py:46
  249.7 1.5 copy-done
  251.2 2.4 fusion
  253.6 51.3 %all-gather.12.cloned.1.call-done = bf16[2048,1536]{0,1:T(8,128)(2,1)} async-done(((bf16[128,1536]{0,1:T(8,128)(2,1)}), bf16[2048,1536]{0,1:T(8,128)(2,1)}) %all-gather.12.cloned.1.call-update) | async-done | bytes 6291472 | tf_op jit(solution)/shard_map/all_gather | solution.py:34
  305.0 16.3 %fusion.36 = (f32[12,128]{1,0:T(8,128)S(1)}, bf16[12,128,2048]{2,1,0:T(8,128)(2,1)}) fusion(f32[12,128,2048]{2,1,0:T(8,128)} %fusion.38, bf16[128,12,128]{0,2,1:T(8,128)(2,1)S(1)} %bitcast.49, bf16[2048,12,128]{0,2,1:T(8,128)(2,1)} %bitcast.47, f32[12,128]{1,0:T(8,128)S(1)} %broadcast_maximum_fusion, f32[12,128,2048]{2,1,0:T(8,128)} %copy-done), kind=kOutput, calls=%fused_computation.42 | convolution fusion | flops 827324928 | bytes 38154240 | tf_op jit(solution)/shard_map/qhd,khd->hqk/dot_general | solution.py:47
  321.3 6.6 %fusion.27 = f32[12,128,128]{1,2,0:T(8,128)S(1)} fusion(bf16[2048,12,128]{0,2,1:T(8,128)(2,1)S(1)} %bitcast.46, f32[12,128,2048]{2,1,0:T(8,128)} %copy-done, f32[12,128]{1,0:T(8,128)S(1)} %broadcast_maximum_fusion), kind=kOutput, calls=%fused_computation.29 | convolution fusion | flops 814743552 | bytes 19666944 | tf_op jit(solution)/shard_map/hqk,khd->hqd/dot_general | solution.py:61
  327.9 10.5 %fusion.22 = f32[128,12,128]{0,2,1:T(8,128)} fusion(bf16[2048,12,128]{0,2,1:T(8,128)(2,1)} %reshape_reshape.3, f32[12,128,2048]{2,1,0:T(8,128)} %copy-done, f32[12,128]{1,0:T(8,128)S(1)} %broadcast_maximum_fusion, f32[128,12]{0,1:T(8,128)S(1)} %bitcast.53), kind=kOutput, calls=%fused_computation.24 | convolution fusion | flops 814940160 | bytes 19673088 | tf_op jit(solution)/shard_map/hqk,khd->hqd/dot_general | solution.py:56
  338.5 6.1 %fusion.19 = f32[128,12,128]{0,2,1:T(8,128)} fusion(f32[12,128,128]{1,2,0:T(8,128)S(1)} %fusion.27, bf16[2048,12,128]{0,2,1:T(8,128)(2,1)} %reshape_reshape.3, bf16[12,128,2048]{2,1,0:T(8,128)(2,1)S(1)} %copy-done.2, f32[128,12,128]{0,2,1:T(8,128)} %fusion.22, f32[128,12]{0,1:T(8,128)S(1)} %bitcast_divide_fusion, f32[128,12]{0,1:T(8,128)S(1)} %bitcast.54), kind=kOutput, calls=%fused_computation.23 | convolution fusion | flops 806092800 | bytes 14954496 | tf_op jit(solution)/shard_map/hqk,khd->hqd/dot_general | solution.py:59
  344.6 1.4 copy.47
  346.0 1.4 copy.39
  347.4 0.1 add_convert_fusion.1
  347.5 11.9 %all_gather.27 = bf16[128,3072]{1,0:T(8,128)(2,1)} all-gather(bf16[128,1536]{1,0:T(8,128)(2,1)S(1)} %add_convert_fusion.1), channel_id=1, replica_groups=mesh['dp'=2,'seq'=16] {'dp'}, dimensions={1}, use_global_device_ids=true | all-gather | bytes 1179648 | tf_op jit(solution)/shard_map/all_gather | solution.py:76
  359.4 0.1 add_convert_fusion.3
  359.5 10.9 %all_gather.22 = bf16[128,3072]{1,0:T(8,128)(2,1)S(1)} all-gather(bf16[128,1536]{1,0:T(8,128)(2,1)S(1)} %add_convert_fusion.3), channel_id=1, replica_groups=mesh['dp'=2,'seq'=16] {'dp'}, dimensions={1}, use_global_device_ids=true | all-gather | bytes 1179648 | tf_op jit(solution)/shard_map/all_gather | solution.py:75
  370.4 48.0 %all-gather.8.cloned.1.call-done = bf16[3072,3584]{1,0:T(8,128)(2,1)} async-done(((bf16[192,3584]{1,0:T(8,128)(2,1)}), bf16[3072,3584]{1,0:T(8,128)(2,1)}) %all-gather.8.cloned.1.call-update) | async-done | bytes 22020112 | tf_op jit(solution)/shard_map/all_gather | solution.py:71
  418.3 11.7 %fusion.37 = f32[128,3584]{1,0:T(8,128)} fusion(bf16[128,3072]{1,0:T(8,128)(2,1)S(1)} %all_gather.22, bf16[3072,3584]{1,0:T(8,128)(2,1)} %all-gather.8.cloned.1.call-done), kind=kOutput, calls=%fused_computation.43 | convolution fusion | flops 2818572288 | bytes 24641536 | tf_op jit(solution)/shard_map/dot_general | solution.py:78
  430.0 3.4 copy-done.1
  433.4 6.5 %fusion.4 = bf16[128,3584]{1,0:T(8,128)(2,1)} fusion(bf16[128,3072]{1,0:T(8,128)(2,1)} %all_gather.27, bf16[3072,3584]{1,0:T(8,128)(2,1)S(1)} %copy-done.1, f32[128,3584]{1,0:T(8,128)} %fusion.37), kind=kOutput, calls=%fused_computation.8 | convolution fusion | flops 2827288576 | bytes 25559040 | tf_op jit(solution)/shard_map/dot_general | solution.py:79
  440.0 93.6 %all-gather.10.cloned.1.call-done = bf16[3584,3072]{1,0:T(8,128)(2,1)} async-done(((bf16[224,3072]{1,0:T(8,128)(2,1)}), bf16[3584,3072]{1,0:T(8,128)(2,1)}) %all-gather.10.cloned.1.call-update) | async-done | bytes 22020112 | tf_op jit(solution)/shard_map/all_gather | solution.py:72
  533.5 11.5 %convolution_convert_fusion = bf16[128,3072]{1,0:T(8,128)(2,1)} fusion(bf16[128,3584]{1,0:T(8,128)(2,1)} %fusion.4, bf16[3584,3072]{1,0:T(8,128)(2,1)} %all-gather.10.cloned.1.call-done), kind=kOutput, calls=%fused_computation.9 | convolution fusion | flops 2818965504 | bytes 23724032 | tf_op jit(solution)/shard_map/dot_general | solution.py:84
  545.0 0.0 reduce-scatter.3.cloned.1.call-start
  545.1 11.7 %convolution_convert_fusion.1 = bf16[128,3072]{1,0:T(8,128)(2,1)} fusion(bf16[3584,3072]{1,0:T(8,128)(2,1)} %all-gather.10.cloned.1.call-done, f32[128,3584]{1,0:T(8,128)S(1)} %copy-done.3), kind=kOutput, calls=%fused_computation.10 | convolution fusion | flops 2823094272 | bytes 24641536 | tf_op jit(solution)/shard_map/dot_general | solution.py:83
  556.8 5.9 reduce-scatter.5.cloned.1.call-done
  562.7 1.8 add_convert_fusion
  564.5 18.0 %reduce-scatter.3.cloned.1.call-done = bf16[128,1536]{1,0:T(8,128)(2,1)} async-done(((bf16[128,3072]{1,0:T(8,128)(2,1)}), bf16[128,1536]{1,0:T(8,128)(2,1)}) %reduce-scatter.3.cloned.1.call-update) | async-done | bytes 393232 | tf_op jit(solution)/shard_map/reduce_scatter | solution.py:86
  582.5 1.8 add_convert_fusion.2
  (31 shorter events, 0.1 us)
Async XLA Ops:
  7.2 195.7 %all-gather.14.cloned.1.call-start = ((), (), s32[]{:S(2)}) async-start(), calls=%async_computation.8 | async-start | bytes 6684672 | tf_op jit(solution)/shard_map/all_gather | solution.py:35
  7.9 230.0 %all-gather.6.cloned.1.call-start = ((), (), s32[]{:S(2)}) async-start(), calls=%async_computation.3 | async-start | bytes 6684672 | tf_op jit(solution)/shard_map/all_gather | solution.py:30
  9.9 295.1 %all-gather.12.cloned.1.call-start = ((), (), s32[]{:S(2)}) async-start(), calls=%async_computation.7 | async-start | bytes 6684672 | tf_op jit(solution)/shard_map/all_gather | solution.py:34
  11.9 406.5 %all-gather.8.cloned.1.call-start = ((), (), s32[]{:S(2)}) async-start(), calls=%async_computation.4 | async-start | bytes 23396352 | tf_op jit(solution)/shard_map/all_gather | solution.py:71
  12.5 521.1 %all-gather.10.cloned.1.call-start = ((), (), s32[]{:S(2)}) async-start(), calls=%async_computation.5 | async-start | bytes 23396352 | tf_op jit(solution)/shard_map/all_gather | solution.py:72
  18.1 7.7 %copy-start.4 = (bf16[128,1536]{1,0:T(8,128)(2,1)S(1)}, bf16[128,1536]{1,0:T(8,128)(2,1)}, u32[]{:S(2)}) copy-start(bf16[128,1536]{1,0:T(8,128)(2,1)} %param.10) | copy-start | bytes 1179652
  18.1 7.9 %copy-start.5 = (bf16[128,1536]{1,0:T(8,128)(2,1)S(1)}, bf16[128,1536]{1,0:T(8,128)(2,1)}, u32[]{:S(2)}) copy-start(bf16[128,1536]{1,0:T(8,128)(2,1)} %param.13) | copy-start | bytes 1179652
  18.1 165.8 %all-to-all-start = ((bf16[16,128,1536]{1,2,0:T(8,128)(2,1)}), bf16[16,128,1536]{1,2,0:T(8,128)(2,1)}, u32[]{:S(2)}, u32[]{:S(2)}) async-start(bf16[16,128,1536]{1,2,0:T(8,128)(2,1)} %stack.2), calls=%async_computation | async-start | bytes 12582912 | tf_op jit(solution)/shard_map/all_to_all | solution.py:32
  25.7 537.0 %reduce-scatter.5.cloned.1.call-start = ((), (), s32[]{:S(2)}) async-start(), calls=%async_computation.9 | async-start | bytes 1179648 | tf_op jit(solution)/shard_map/reduce_scatter | solution.py:89
  237.9 4.9 slice-start
  237.9 4.9 slice-start.1
  242.8 8.4 %copy-start = (f32[12,128,2048]{2,1,0:T(8,128)}, f32[12,128,2048]{2,1,0:T(8,128)S(1)}, u32[]{:S(2)}) copy-start(f32[12,128,2048]{2,1,0:T(8,128)S(1)} %get-tuple-element.3) | copy-start | bytes 37748740
  251.2 70.1 %slice-start.2 = ((s8[6291456]{0:T(1024)(128)(4,1)}), s8[2097152]{0:T(1024)(128)(4,1)S(1)}, s32[]{:S(2)}) async-start(s8[6291456]{0:T(1024)(128)(4,1)} %bitcast.44), calls=%async_computation.12 | async-start | bytes 4194304
  305.0 16.3 %slice-start.3 = ((s8[6291456]{0:T(1024)(128)(4,1)}), s8[4194304]{0:T(1024)(128)(4,1)S(1)}, s32[]{:S(2)}) async-start(s8[6291456]{0:T(1024)(128)(4,1)} %bitcast.44), calls=%async_computation.13 | async-start | bytes 8388608
  327.9 10.6 %copy-start.2 = (bf16[12,128,2048]{2,1,0:T(8,128)(2,1)S(1)}, bf16[12,128,2048]{2,1,0:T(8,128)(2,1)}, u32[]{:S(2)}) copy-start(bf16[12,128,2048]{2,1,0:T(8,128)(2,1)} %get-tuple-element.5) | copy-start | bytes 18874372
  338.5 9.0 %copy-start.6 = (bf16[128,1536]{1,0:T(8,128)(2,1)S(1)}, bf16[128,1536]{1,0:T(8,128)(2,1)}, u32[]{:S(2)}) copy-start(bf16[128,1536]{1,0:T(8,128)(2,1)} %param.17) | copy-start | bytes 1179652
  338.5 20.9 %copy-start.7 = (bf16[128,1536]{1,0:T(8,128)(2,1)S(1)}, bf16[128,1536]{1,0:T(8,128)(2,1)}, u32[]{:S(2)}) copy-start(bf16[128,1536]{1,0:T(8,128)(2,1)} %param.16) | copy-start | bytes 1179652
  418.3 15.1 %copy-start.1 = (bf16[3072,3584]{1,0:T(8,128)(2,1)S(1)}, bf16[3072,3584]{1,0:T(8,128)(2,1)}, u32[]{:S(2)}) copy-start(bf16[3072,3584]{1,0:T(8,128)(2,1)} %all-gather.8.cloned.1.call-done) | copy-start | bytes 66060292
  440.0 105.1 %copy-start.3 = (f32[128,3584]{1,0:T(8,128)S(1)}, f32[128,3584]{1,0:T(8,128)}, u32[]{:S(2)}) copy-start(f32[128,3584]{1,0:T(8,128)} %fusion.37) | copy-start | bytes 5505028
  545.0 37.5 %reduce-scatter.3.cloned.1.call-start = ((), (), s32[]{:S(2)}) async-start(), calls=%async_computation.6 | async-start | bytes 1179648 | tf_op jit(solution)/shard_map/reduce_scatter | solution.py:86
Sparse Core Ops, SparseCore 0:
  10.3 144.8 all-gather.13
  157.9 80.0 all-gather.5
  240.7 64.2 all-gather.11
  306.4 111.8 all-gather.7
  419.8 113.6 all-gather.9
  545.1 17.4 reduce-scatter.4
  564.9 17.5 reduce-scatter.2
